TPU v7x, 32 devices: a whole 2x2x4 slice. The times are simulated.
32 devices in a mesh: track: 8 (over y, x, core), cols: 4 (over z).
Axes of the slice: x: 2, y: 2, z: 4, core: 2. Of those that a mesh axis runs over, the one named last changes fastest.
Arguments:
- design: bfloat16 [4096, 4096], P('track', 'cols'), may hold values from -0.09375 to 0.09375
- seg_start: int32 [4096], P('track'), may hold values from 0 to 4095, as said below
- seg_table: int32 [4096], P('track'), may hold values from 0 to 7, as said below
- taps: bfloat16 [8, 97], replicated, may hold values from -1.25 to 1.25
- ridge: float32 [4096], replicated, may hold values from 0.3 to 3
- col_perm: int32 [4096], replicated, may hold values from 0 to 4095, each once
Outputs:
- normals: float32 [4096, 4096], P('track', 'cols')
- factor: float32 [4096, 1024], P('track', 'cols')
Inputs may be any that keep to these rules, and one draw needn't show every extreme that they name: seg_start[r] is the first row of the run of consecutive rows that holds row r; it never exceeds r, row 0 starts a run, the last row starts a run of its own, and all rows of a run carry the same value. `seg_table`: all rows with the same seg_start carry the same table. `col_perm`: each of 0 to 4095 once.
All inputs are finite; a program needn't handle non-finite values.
Results may differ from a plain program's by a relative error of at most 0.0019.
Values may be sent and summed in bfloat16 or wider, within the bound.
A program may use at most 64 MiB of HBM per device.

v0:
```python
import jax
import jax.numpy as jnp
from jax import lax
from jax.sharding import PartitionSpec as P

PANEL = 1024


def shifted(shard, axis, by):
    devices = lax.axis_size(axis)
    pairs = [(i, i + by) for i in range(devices) if 0 <= i + by < devices]
    return lax.ppermute(shard, axis, pairs)


def filter_rows(local, ext_top, seg_start, seg_table, taps, first_row):
    halo_rows = taps.shape[1] - 1
    row_count, columns = local.shape
    block = min(512, row_count)
    blocks = row_count // block
    extended = jnp.concatenate([ext_top, local], axis=0)
    upper = extended[:row_count].reshape(blocks, block, columns)
    lower_part = local.reshape(blocks, block, columns)[:, block - halo_rows :, :]
    windows = jnp.concatenate([upper, lower_part], axis=1)
    onehot = (seg_table[:, None] == jnp.arange(taps.shape[0], dtype=jnp.int32)[None, :]).astype(
        jnp.float32
    )
    row_taps = jnp.dot(onehot, taps.astype(jnp.float32), precision=lax.Precision.HIGHEST)
    flipped = row_taps[:, ::-1].reshape(blocks, block, halo_rows + 1)
    span = block + halo_rows
    padded = jnp.pad(flipped, ((0, 0), (0, 0), (0, span - halo_rows)))
    skewed = padded.reshape(blocks, block * (span + 1))[:, : block * span].reshape(
        blocks, block, span
    )
    offsets = (jnp.arange(blocks, dtype=jnp.int32) * block)[:, None, None]
    col_rows = first_row + offsets - halo_rows + jnp.arange(span, dtype=jnp.int32)[None, None, :]
    starts = seg_start.reshape(blocks, block)[:, :, None]
    coefs = jnp.where(col_rows >= starts, skewed, 0.0).astype(jnp.bfloat16)
    summed = jnp.einsum("brj,bjc->brc", coefs, windows, preferred_element_type=jnp.float32)
    return summed.reshape(row_count, columns).astype(jnp.bfloat16)


def body(design, seg_start, seg_table, taps, ridge, col_perm):
    row_count, width_dev = design.shape
    halo_rows = taps.shape[1] - 1
    track_index = lax.axis_index("track")
    col_index = lax.axis_index("cols")
    ext_top = shifted(design[row_count - halo_rows :], "track", 1)
    filtered = filter_rows(design, ext_top, seg_start, seg_table, taps, track_index * row_count)
    gathered = lax.all_gather(filtered, "cols", axis=1, tiled=True)
    row_blk = gathered.shape[1] // lax.axis_size("track")
    panel_blk = PANEL // lax.axis_size("cols")
    panel_ids = col_perm[:PANEL]
    sums = lax.psum_scatter(
        lax.dot_general(
            gathered, filtered, (((0,), (0,)), ((), ())), preferred_element_type=jnp.float32
        ),
        "track",
        scatter_dimension=0,
        tiled=True,
    )
    row_ids = track_index * row_blk + jnp.arange(row_blk, dtype=jnp.int32)
    col_ids = col_index * width_dev + jnp.arange(width_dev, dtype=jnp.int32)
    row_ridge = lax.dynamic_slice_in_dim(ridge, track_index * row_blk, row_blk)
    normals = sums + jnp.where(row_ids[:, None] == col_ids[None, :], row_ridge[:, None], 0.0)
    whole_rows = lax.all_gather(normals, "cols", axis=1, tiled=True)
    panel_rows = jnp.take(whole_rows, panel_ids, axis=1)
    own_cols = lax.dynamic_slice_in_dim(panel_rows, col_index * panel_blk, panel_blk, 1)
    selector = (panel_ids[:, None] == row_ids[None, :]).astype(jnp.float32)
    block_part = jnp.dot(selector, own_cols, precision=lax.Precision.HIGHEST)
    panel_cols = lax.psum(block_part, "track")
    whole_block = lax.all_gather(panel_cols, "cols", axis=1, tiled=True)
    lower = jnp.linalg.cholesky(whole_block)
    solved = lax.linalg.triangular_solve(
        lower, panel_rows, left_side=False, lower=True, transpose_a=True
    )
    factor = lax.dynamic_slice_in_dim(solved, col_index * panel_blk, panel_blk, 1)
    return (normals, factor)


def solution(mesh):
    in_specs = (P("track", "cols"), P("track"), P("track"), P(), P(), P())
    out_specs = (P("track", "cols"), P("track", "cols"))
    return jax.shard_map(body, mesh=mesh, in_specs=in_specs, out_specs=out_specs, check_vma=False)
```

profile of v0, /device:TPU:0, one launch (start us, length us, event | category | flops | bytes accessed | tf_op | source)
XLA Modules:
  0.0 901.8 jit_solution(4148739313141080950)
XLA Ops:
  8.2 2.4 collective-permute-start
  12.0 1.4 reshape.167
  13.6 2.9 ge.37
  16.7 2.9 ge.39
  19.6 13.3 %fusion.6 = bf16[311296]{0:T(1024)(128)(2,1)S(1)} fusion(bf16[1,311808]{1,0:T(2,128)(2,1)S(1)} %reshape.167, s32[1,311296]{1,0:T(1,128)} %ge.37, s32[1,311296]{1,0:T(1,128)} %ge.39), kind=kLoop, calls=%fused_computation.17 | loop fusion | flops 622592 | bytes 3735552 | tf_op jit(solution)/shard_map/convert_element_type | solution.py:37
  34.8 2.0 convolution_convert_fusion
  37.3 82.9 %all-gather.4.cloned.1.call-done = bf16[512,4096]{1,0:T(8,128)(2,1)} async-done(((bf16[512,1024]{1,0:T(8,128)(2,1)}), bf16[512,4096]{1,0:T(8,128)(2,1)}) %all-gather.4.cloned.1.call-update) | async-done | bytes 4194320 | tf_op jit(solution)/shard_map/all_gather | solution.py:49
  120.3 12.8 %fusion.78 = f32[4096,1024]{1,0:T(8,128)} fusion(bf16[512,4096]{1,0:T(8,128)(2,1)} %all-gather.4.cloned.1.call-done, bf16[512,1024]{1,0:T(8,128)(2,1)} %convolution_convert_fusion), kind=kOutput, calls=%fused_computation.185 | convolution fusion | flops 4294967296 | bytes 22020096 | tf_op jit(solution)/shard_map/dot_general | solution.py:54
  133.9 114.0 %reduce-scatter.2.cloned.1.call-done = f32[512,1024]{1,0:T(8,128)} async-done(((f32[4096,1024]{1,0:T(8,128)}), f32[512,1024]{1,0:T(8,128)}) %reduce-scatter.2.cloned.1.call-update) | async-done | bytes 2097168 | tf_op jit(solution)/shard_map/reduce_scatter | solution.py:53
  247.9 3.2 select_add_fusion
  251.8 149.0 %all-gather.6.cloned.1.call-done = f32[512,4096]{1,0:T(8,128)} async-done(((f32[512,1024]{1,0:T(8,128)}), f32[512,4096]{1,0:T(8,128)}) %all-gather.6.cloned.1.call-update) | async-done | bytes 8388624 | tf_op jit(solution)/shard_map/all_gather | solution.py:65
  400.9 9.0 copy.13
  409.9 7.4 gather_fusion
  417.5 2.2 fusion.1
  419.8 55.0 %all-reduce.4.cloned.1.call-done = f32[1024,256]{0,1:T(8,128)} async-done(((f32[1024,256]{0,1:T(8,128)}), f32[1024,256]{0,1:T(8,128)}) %all-reduce.4.cloned.1.call-update) | async-done | bytes 1048592 | tf_op jit(solution)/shard_map/psum | solution.py:70
  474.8 1.6 fusion.95
  476.4 79.8 %all-gather.8.cloned.1.call-done = f32[1024,1024]{0,1:T(8,128)} async-done(((f32[1024,256]{0,1:T(8,128)}), f32[1024,1024]{0,1:T(8,128)}) %all-gather.8.cloned.1.call-update) | async-done | bytes 4194320 | tf_op jit(solution)/shard_map/all_gather | solution.py:71
  556.2 5.5 copy.15
  561.7 4.4 fusion
  566.2 1.9 copy-done.2
  568.1 11.7 %cholesky.223 = f32[128,128]{1,0:T(8,128)S(1)} custom-call(f32[128,128]{1,0:T(8,128)S(1)} %cholesky.580), custom_call_target="Cholesky" | custom-call | tf_op jit(solution)/shard_map/jit(cholesky)/cholesky | solution.py:72
  579.8 2.5 cholesky.255
  582.3 9.8 %custom-call.62 = f32[1,128,128]{1,2,0:T(8,128)S(1)} custom-call(f32[1,128,128]{2,1,0:T(8,128)S(1)} %get-tuple-element.70), custom_call_target="InvertDiagBlocksLowerTriangular" | custom-call | tf_op jit(solution)/shard_map/jit(cholesky)/cholesky | solution.py:72
  592.2 2.4 constant_dynamic-update-slice_fusion.30
  594.5 1.5 convolution_subtract_fusion
  596.1 11.9 %cholesky.244 = f32[128,128]{1,0:T(8,128)S(1)} custom-call(f32[128,128]{1,0:T(8,128)S(1)} %cholesky.584), custom_call_target="Cholesky" | custom-call | tf_op jit(solution)/shard_map/jit(cholesky)/cholesky | solution.py:72
  608.6 9.8 %custom-call.63 = f32[1,128,128]{1,2,0:T(8,128)S(1)} custom-call(f32[1,128,128]{2,1,0:T(8,128)S(1)} %get-tuple-element.67), custom_call_target="InvertDiagBlocksLowerTriangular" | custom-call | tf_op jit(solution)/shard_map/jit(cholesky)/cholesky | solution.py:72
  618.5 1.2 convolution_dynamic-update-slice_fusion
  619.7 2.1 convolution_subtract_fusion.1
  621.8 11.7 %cholesky.468 = f32[128,128]{1,0:T(8,128)S(1)} custom-call(f32[128,128]{1,0:T(8,128)S(1)} %cholesky.589), custom_call_target="Cholesky" | custom-call | tf_op jit(solution)/shard_map/jit(cholesky)/cholesky | solution.py:72
  634.9 9.8 %custom-call.64 = f32[1,128,128]{1,2,0:T(8,128)S(1)} custom-call(f32[1,128,128]{2,1,0:T(8,128)S(1)} %get-tuple-element.64), custom_call_target="InvertDiagBlocksLowerTriangular" | custom-call | tf_op jit(solution)/shard_map/jit(cholesky)/cholesky | solution.py:72
  644.7 1.2 convolution_dynamic-update-slice_fusion.1
  645.8 2.4 convolution_subtract_fusion.2
  648.2 12.1 %cholesky.487 = f32[128,128]{1,0:T(8,128)S(1)} custom-call(f32[128,128]{1,0:T(8,128)S(1)} %cholesky.594), custom_call_target="Cholesky" | custom-call | tf_op jit(solution)/shard_map/jit(cholesky)/cholesky | solution.py:72
  661.6 9.8 %custom-call.65 = f32[1,128,128]{1,2,0:T(8,128)S(1)} custom-call(f32[1,128,128]{2,1,0:T(8,128)S(1)} %get-tuple-element.61), custom_call_target="InvertDiagBlocksLowerTriangular" | custom-call | tf_op jit(solution)/shard_map/jit(cholesky)/cholesky | solution.py:72
  672.5 2.3 convolution_subtract_fusion.10
  674.9 11.7 %cholesky.506 = f32[128,128]{1,0:T(8,128)S(1)} custom-call(f32[128,128]{1,0:T(8,128)S(1)} %cholesky.599), custom_call_target="Cholesky" | custom-call | tf_op jit(solution)/shard_map/jit(cholesky)/cholesky | solution.py:72
  687.9 9.9 %custom-call.66 = f32[1,128,128]{1,2,0:T(8,128)S(1)} custom-call(f32[1,128,128]{2,1,0:T(8,128)S(1)} %get-tuple-element.58), custom_call_target="InvertDiagBlocksLowerTriangular" | custom-call | tf_op jit(solution)/shard_map/jit(cholesky)/cholesky | solution.py:72
  698.9 2.3 convolution_subtract_fusion.11
  701.2 11.7 %cholesky.526 = f32[128,128]{1,0:T(8,128)S(1)} custom-call(f32[128,128]{1,0:T(8,128)S(1)} %cholesky.604), custom_call_target="Cholesky" | custom-call | tf_op jit(solution)/shard_map/jit(cholesky)/cholesky | solution.py:72
  714.2 9.8 %custom-call.67 = f32[1,128,128]{1,2,0:T(8,128)S(1)} custom-call(f32[1,128,128]{2,1,0:T(8,128)S(1)} %get-tuple-element.55), custom_call_target="InvertDiagBlocksLowerTriangular" | custom-call | tf_op jit(solution)/shard_map/jit(cholesky)/cholesky | solution.py:72
  724.9 2.0 convolution_subtract_fusion.12
  727.0 11.9 %cholesky.546 = f32[128,128]{1,0:T(8,128)S(1)} custom-call(f32[128,128]{1,0:T(8,128)S(1)} %cholesky.609), custom_call_target="Cholesky" | custom-call | tf_op jit(solution)/shard_map/jit(cholesky)/cholesky | solution.py:72
  740.2 9.8 %custom-call.68 = f32[1,128,128]{1,2,0:T(8,128)S(1)} custom-call(f32[1,128,128]{2,1,0:T(8,128)S(1)} %get-tuple-element.52), custom_call_target="InvertDiagBlocksLowerTriangular" | custom-call | tf_op jit(solution)/shard_map/jit(cholesky)/cholesky | solution.py:72
  750.8 1.8 convolution_subtract_fusion.13
  752.6 11.7 %cholesky.564 = f32[128,128]{1,0:T(8,128)S(1)} custom-call(f32[128,128]{1,0:T(8,128)S(1)} %convolution_subtract_fusion.13), custom_call_target="Cholesky" | custom-call | tf_op jit(solution)/shard_map/jit(cholesky)/cholesky | solution.py:72
  771.4 4.9 select_select_fusion
  776.3 22.8 %while.1 = (s32[]{:T(128)}, f32[1024,1024]{1,0:T(8,128)}, s32[8,2]{0,1:T(2,128)S(1)}, f32[8,128,128]{2,1,0:T(8,128)S(1)}, s32[]{:T(128)}) while((s32[]{:T(128)}, f32[1024,1024]{1,0:T(8,128)}, s32[8,2]{0,1:T(2,128)S(1)}, f32[8,128,128]{2,1,0:T(8,128)S(1)}, s32[]{:T(128)}) %tuple.64), condition=%wide.while_cond, body=%wide.while_body.sunk | while | flops 2 | bytes 131189 | solution.py:73
  777.0 2.2 bitcast_dynamic-update-slice_fusion.2
  779.8 2.2 bitcast_dynamic-update-slice_fusion.2
  782.7 2.2 bitcast_dynamic-update-slice_fusion.2
  785.6 2.2 bitcast_dynamic-update-slice_fusion.2
  788.4 2.2 bitcast_dynamic-update-slice_fusion.2
  791.3 2.2 bitcast_dynamic-update-slice_fusion.2
  794.1 2.2 bitcast_dynamic-update-slice_fusion.2
  797.0 2.2 bitcast_dynamic-update-slice_fusion.2
  799.2 78.8 %custom-call.69 = f32[8,128,128]{1,2,0:T(8,128)S(1)} custom-call(f32[8,128,128]{2,1,0:T(8,128)S(1)} %get-tuple-element.9), custom_call_target="InvertDiagBlocksLowerTriangular" | custom-call | tf_op jit(solution)/shard_map/triangular_solve | solution.py:73
  878.5 1.2 convolution_subtract_fusion.6
  880.2 1.3 convolution_subtract_fusion.5
  882.1 1.6 convolution_subtract_fusion.8
  884.1 1.7 convolution_subtract_fusion.9
  886.3 1.9 convolution_subtract_fusion.4
  888.6 2.0 convolution_subtract_fusion.7
  891.1 2.2 convolution_subtract_fusion.3
  (96 shorter events, 29.8 us)
Async XLA Ops:
  7.2 3.4 copy-start
  7.2 113.1 %all-gather.4.cloned.1.call-start = ((), (), s32[]{:S(2)}) async-start(), calls=%async_computation.1 | async-start | bytes 5242880 | tf_op jit(solution)/shard_map/all_gather | solution.py:49
  8.2 26.6 %collective-permute-start = (bf16[96,1024]{1,0:T(8,128)(2,1)S(1)}, bf16[96,1024]{1,0:T(8,128)(2,1)S(1)}, u32[]{:S(2)}, u32[]{:S(2)}) collective-permute-start(bf16[96,1024]{1,0:T(8,128)(2,1)S(1)} %slice.239), channel_id=1, source_target_pairs={{0,4},{4,8},{8,12},{12,16},{16,20},{20,24},{24,28},{1,5},{5,9},{9,... | collective-permute-start | bytes 589832 | tf_op jit(solution)/shard_map/ppermute | solution.py:12
  13.5 3.0 copy-start.6
  32.8 1.9 copy-start.4
  36.8 211.1 %reduce-scatter.2.cloned.1.call-start = ((), (), s32[]{:S(2)}) async-start(), calls=%async_computation.2 | async-start | bytes 18874368 | tf_op jit(solution)/shard_map/reduce_scatter | solution.py:53
  133.1 267.8 %all-gather.6.cloned.1.call-start = ((), (), s32[]{:S(2)}) async-start(), calls=%async_computation.3 | async-start | bytes 10485760 | tf_op jit(solution)/shard_map/all_gather | solution.py:65
  251.1 0.7 copy-start.5
  251.1 223.6 %all-reduce.4.cloned.1.call-start = ((), (), s32[]{:S(2)}) async-start(), calls=%async_computation.4 | async-start | bytes 2097152 | tf_op jit(solution)/shard_map/psum | solution.py:70
  419.7 136.5 %all-gather.8.cloned.1.call-start = ((), (), s32[]{:S(2)}) async-start(), calls=%async_computation.5 | async-start | bytes 5242880 | tf_op jit(solution)/shard_map/all_gather | solution.py:71
  566.2 1.9 copy-start.2
  771.4 106.7 %copy-start.3 = (f32[512,1024]{0,1:T(8,128)S(1)}, f32[512,1024]{0,1:T(8,128)}, u32[]{:S(2)}) copy-start(f32[512,1024]{0,1:T(8,128)} %fusion.95) | copy-start | bytes 6291460
  891.1 3.7 copy-start.1
Sparse Core Ops, SparseCore 0:
  36.9 83.2 all-gather.3
  133.2 114.6 reduce-scatter.1
  251.3 149.5 all-gather.5
  419.9 54.8 all-reduce.3
  476.2 79.9 all-gather.7
where the time goes:
time: 912 us; the launch traced here: 902 us
  waiting for transfers between devices  481 us (53%)
  other arithmetic  279 us (31%)
  local copies, waits for them, and re-layouts  62.3 us (7%)
  matrix products  56.6 us (6%)
  between operations  19.7 us (2%)
    another operation x30, other arithmetic, body(): lower = jnp.linalg.cholesky(whole_block)  172 us
    all_gather x1, waiting for transfers between devices, body(): whole_rows = lax.all_gather(normals, 'cols', axis=1, tiled=True)  149 us
    reduce_scatter x1, waiting for transfers between devices, body(): lax.psum_scatter(lax.dot_general(gathered, filtered, (((0,), (0,)), ((),...  114 us
    another operation x3, other arithmetic, body(): lax.linalg.triangular_solve(lower, panel_rows, left_side=False, lower=Tru...  83.8 us
    all_gather x1, waiting for transfers between devices, body(): gathered = lax.all_gather(filtered, 'cols', axis=1, tiled=True)  82.9 us
    all_gather x1, waiting for transfers between devices, body(): whole_block = lax.all_gather(panel_cols, 'cols', axis=1, tiled=True)  79.8 us
    psum x1, waiting for transfers between devices, body(): panel_cols = lax.psum(block_part, 'track')  55 us
    another operation x14, matrix products, body(): lower = jnp.linalg.cholesky(whole_block)  23.1 us
  transfers between devices with their start and end apart: 6, of which 5 were waited for; matrix products, arithmetic and copies ran while one was open for 3% of the time, Pallas kernels for 0%

commit v1 on v0

--- a/solution.py
+++ b/solution.py
@@ -1,9 +1,13 @@
 import jax
 import jax.numpy as jnp
 from jax import lax
+from jax.experimental import pallas as pl
+from jax.experimental.pallas import tpu as pltpu
 from jax.sharding import PartitionSpec as P
 
 PANEL = 1024
+TILE = 128
+SUB = 8
 
 
 def shifted(shard, axis, by):
@@ -39,41 +43,194 @@
     return summed.reshape(row_count, columns).astype(jnp.bfloat16)
 
 
+def split(x):
+    hi = x.astype(jnp.bfloat16)
+    lo = (x - hi.astype(jnp.float32)).astype(jnp.bfloat16)
+    return hi, lo
+
+
+def dot_nt(a, b):
+    a_hi, a_lo = a
+    b_hi, b_lo = b
+    return lax.dot_general(
+        jnp.concatenate([a_hi, a_hi, a_lo], axis=1),
+        jnp.concatenate([b_hi, b_lo, b_hi], axis=1),
+        (((1,), (1,)), ((), ())),
+        preferred_element_type=jnp.float32,
+    )
+
+
+def tile_inverse_factor(work, linv):
+    lane_shape = (SUB, TILE)
+    sub_id = lax.broadcasted_iota(jnp.int32, lane_shape, 0)
+    for g in range(TILE // SUB):
+        base = g * SUB
+        rows = work[base : base + SUB, :]
+        left, right = rows[:, :TILE], rows[:, TILE:]
+        cols = [
+            jnp.broadcast_to(left[:, base + k : base + k + 1], lane_shape) for k in range(SUB)
+        ]
+        s = [
+            [jnp.broadcast_to(cols[k][i : i + 1, :], lane_shape) for k in range(i + 1)]
+            for i in range(SUB)
+        ]
+        inv_diag = []
+        for k in range(SUB):
+            r = lax.rsqrt(s[k][k])
+            inv_diag.append(r)
+            for i in range(k + 1, SUB):
+                s[i][k] = s[i][k] * r
+            for i in range(k + 1, SUB):
+                for j in range(k + 1, i + 1):
+                    s[i][j] = s[i][j] - s[i][k] * s[j][k]
+        x = [[None] * SUB for _ in range(SUB)]
+        for j in range(SUB):
+            x[j][j] = inv_diag[j]
+            for i in range(j + 1, SUB):
+                total = s[i][j] * x[j][j]
+                for m in range(j + 1, i):
+                    total = total + s[i][m] * x[m][j]
+                x[i][j] = -inv_diag[i] * total
+        new_left = new_right = None
+        for k in range(SUB):
+            col = jnp.zeros(lane_shape, jnp.float32)
+            for i in range(k, SUB):
+                col = jnp.where(sub_id == i, x[i][k], col)
+            term_l = col * jnp.broadcast_to(left[k : k + 1, :], lane_shape)
+            term_r = col * jnp.broadcast_to(right[k : k + 1, :], lane_shape)
+            new_left = term_l if new_left is None else new_left + term_l
+            new_right = term_r if new_right is None else new_right + term_r
+        linv[base : base + SUB, :] = new_right
+        rest = base + SUB
+        if rest < TILE:
+            both = jnp.concatenate([new_left, new_right], axis=1)
+            hi = both.astype(jnp.bfloat16).astype(jnp.float32)
+            lo = both - hi
+            pad = jnp.zeros_like(hi)
+            lhs = jnp.concatenate(
+                [hi[:, :TILE], hi[:, :TILE], lo[:, :TILE], pad[:, :TILE]], axis=0
+            ).astype(jnp.bfloat16)
+            rhs = jnp.concatenate([hi, lo, hi, pad], axis=0).astype(jnp.bfloat16)
+            update = lax.dot_general(
+                lhs, rhs, (((0,), (0,)), ((), ())), preferred_element_type=jnp.float32
+            )
+            work[rest:, :] = work[rest:, :] - update[rest:, :]
+
+
+def factor_kernel(a_ref, out_ref, held, work, linv):
+    size = a_ref.shape[0]
+    tiles = size // TILE
+    for j in range(tiles):
+        held[j] = a_ref[:, j * TILE : (j + 1) * TILE]
+    row = lax.broadcasted_iota(jnp.int32, (TILE, TILE), 0)
+    lane = lax.broadcasted_iota(jnp.int32, (TILE, TILE), 1)
+    eye = (row == lane).astype(jnp.float32)
+    all_rows = lax.broadcasted_iota(jnp.int32, (size, TILE), 0)
+
+    def step(k, carry):
+        here = pl.ds(pl.multiple_of(k * TILE, TILE), TILE)
+        work[:, :TILE] = held[k, here, :]
+        work[:, TILE:] = eye
+        tile_inverse_factor(work, linv)
+        held[k, here, :] = eye
+        column = dot_nt(split(held[k]), split(linv[...]))
+        held[k] = column
+        out_ref[:, here] = jnp.where(all_rows < (k + 1) * TILE, column, 0.0)
+        parts = split(column)
+
+        def update(j, inner):
+            there = pl.ds(pl.multiple_of(j * TILE, TILE), TILE)
+            other = split(held[k, there, :])
+            held[j, here, :] = jnp.zeros((TILE, TILE), jnp.float32)
+            held[j] = held[j] - dot_nt(parts, other)
+            return inner
+
+        lax.fori_loop(k + 1, tiles, update, 0)
+        return carry
+
+    lax.fori_loop(0, tiles, step, 0)
+
+
+def inverse_factor_transposed(block, interpret=False):
+    size = block.shape[0]
+    return pl.pallas_call(
+        factor_kernel,
+        out_shape=jax.ShapeDtypeStruct((size, size), jnp.float32),
+        in_specs=[pl.BlockSpec(memory_space=pltpu.VMEM)],
+        out_specs=pl.BlockSpec(memory_space=pltpu.VMEM),
+        scratch_shapes=[
+            pltpu.VMEM((size // TILE, size, TILE), jnp.float32),
+            pltpu.VMEM((TILE, 2 * TILE), jnp.float32),
+            pltpu.VMEM((TILE, TILE), jnp.float32),
+        ],
+        compiler_params=pltpu.CompilerParams(vmem_limit_bytes=40 * 1024 * 1024),
+        cost_estimate=pl.CostEstimate(
+            flops=60_000_000_000, bytes_accessed=8 * size * size, transcendentals=size
+        ),
+        interpret=interpret,
+    )(block)
+
+
 def body(design, seg_start, seg_table, taps, ridge, col_perm):
     row_count, width_dev = design.shape
     halo_rows = taps.shape[1] - 1
+    track_size = lax.axis_size("track")
+    cols_size = lax.axis_size("cols")
     track_index = lax.axis_index("track")
     col_index = lax.axis_index("cols")
     ext_top = shifted(design[row_count - halo_rows :], "track", 1)
     filtered = filter_rows(design, ext_top, seg_start, seg_table, taps, track_index * row_count)
     gathered = lax.all_gather(filtered, "cols", axis=1, tiled=True)
-    row_blk = gathered.shape[1] // lax.axis_size("track")
-    panel_blk = PANEL // lax.axis_size("cols")
+    slab = gathered.shape[1]
+    row_blk = slab // track_size
+    panel_blk = PANEL // cols_size
     panel_ids = col_perm[:PANEL]
+    own_ids = lax.dynamic_slice_in_dim(panel_ids, col_index * panel_blk, panel_blk)
+
+    chosen = (jnp.arange(slab, dtype=jnp.int32)[:, None] == panel_ids[None, :]).astype(jnp.bfloat16)
+    panel_filtered = jnp.dot(gathered, chosen, preferred_element_type=jnp.float32).astype(
+        jnp.bfloat16
+    )
+    own_filtered = lax.dynamic_slice_in_dim(panel_filtered, col_index * panel_blk, panel_blk, 1)
+    contract = (((0,), (0,)), ((), ()))
+
+    part = lax.dot_general(
+        panel_filtered, own_filtered, contract, preferred_element_type=jnp.float32
+    )
+    piece = lax.psum_scatter(part, "track", scatter_dimension=0, tiled=True)
+    pieces = lax.all_gather(piece, ("track", "cols"), axis=0)
+    block = (
+        pieces.reshape(track_size, cols_size, PANEL // track_size, panel_blk)
+        .transpose(0, 2, 1, 3)
+        .reshape(PANEL, PANEL)
+    )
+    panel_ridge = jnp.take(ridge, panel_ids)
+    ids = jnp.arange(PANEL, dtype=jnp.int32)
+    block = block + jnp.where(ids[:, None] == ids[None, :], panel_ridge[:, None], 0.0)
+
+    gathered, filtered, own_filtered, block = lax.optimization_barrier(
+        (gathered, filtered, own_filtered, block)
+    )
+    inverse_t = inverse_factor_transposed(block)
+    row_ids = track_index * row_blk + jnp.arange(row_blk, dtype=jnp.int32)
+    row_ridge = lax.dynamic_slice_in_dim(ridge, track_index * row_blk, row_blk)
+
+    own_part = lax.dot_general(gathered, own_filtered, contract, preferred_element_type=jnp.float32)
+    own_cols = lax.psum_scatter(own_part, "track", scatter_dimension=0, tiled=True)
+    own_cols = own_cols + jnp.where(row_ids[:, None] == own_ids[None, :], row_ridge[:, None], 0.0)
+    panel_rows = lax.all_gather(own_cols, "cols", axis=1, tiled=True)
+
     sums = lax.psum_scatter(
-        lax.dot_general(
-            gathered, filtered, (((0,), (0,)), ((), ())), preferred_element_type=jnp.float32
-        ),
+        lax.dot_general(gathered, filtered, contract, preferred_element_type=jnp.float32),
         "track",
         scatter_dimension=0,
         tiled=True,
     )
-    row_ids = track_index * row_blk + jnp.arange(row_blk, dtype=jnp.int32)
     col_ids = col_index * width_dev + jnp.arange(width_dev, dtype=jnp.int32)
-    row_ridge = lax.dynamic_slice_in_dim(ridge, track_index * row_blk, row_blk)
     normals = sums + jnp.where(row_ids[:, None] == col_ids[None, :], row_ridge[:, None], 0.0)
-    whole_rows = lax.all_gather(normals, "cols", axis=1, tiled=True)
-    panel_rows = jnp.take(whole_rows, panel_ids, axis=1)
-    own_cols = lax.dynamic_slice_in_dim(panel_rows, col_index * panel_blk, panel_blk, 1)
-    selector = (panel_ids[:, None] == row_ids[None, :]).astype(jnp.float32)
-    block_part = jnp.dot(selector, own_cols, precision=lax.Precision.HIGHEST)
-    panel_cols = lax.psum(block_part, "track")
-    whole_block = lax.all_gather(panel_cols, "cols", axis=1, tiled=True)
-    lower = jnp.linalg.cholesky(whole_block)
-    solved = lax.linalg.triangular_solve(
-        lower, panel_rows, left_side=False, lower=True, transpose_a=True
-    )
-    factor = lax.dynamic_slice_in_dim(solved, col_index * panel_blk, panel_blk, 1)
+
+    own_inverse = lax.dynamic_slice_in_dim(inverse_t, col_index * panel_blk, panel_blk, 1)
+    factor = jnp.dot(panel_rows, own_inverse, precision=lax.Precision.HIGHEST)
     return (normals, factor)
 
 

time: 912 us -> 467 us (0.51); the launches traced: 902 us -> 466 us
  other arithmetic: 279 us -> 22.2 us
  waiting for transfers between devices: 481 us -> 309 us
  Pallas kernels: 0 us -> 61.5 us
  local copies, waits for them, and re-layouts: 62.3 us -> 27.2 us
  matrix products: 56.6 us -> 28.9 us
    another operation x33 -> x0, other arithmetic: 256 us -> none  [the longest x30 172 us: body(): lower = jnp.linalg.cholesky(whole_block)]
    all_gather x2, waiting for transfers between devices: 229 us -> 58.4 us  [the longest x1 58.4 us: body(): pieces = lax.all_gather(piece, ('track', 'cols'), axis=0)]
    pallas_call x0 -> x1, Pallas kernels: none -> 61.5 us  [inverse_factor_transposed(): pl.pallas_call(factor_kernel, out_shape=jax.ShapeDtypeStruct((size, size)...]
    psum x1 -> x0, waiting for transfers between devices: 55 us -> none  [body(): panel_cols = lax.psum(block_part, 'track')]
    reduce_scatter x1 -> x3, waiting for transfers between devices: 114 us -> 168 us  [the longest x1 83.2 us: body(): lax.psum_scatter(lax.dot_general(gathered, filtered, contract, preferred_...]
    another operation x29 -> x0, matrix products: 38.7 us -> none  [the longest x14 23.1 us: body(): lower = jnp.linalg.cholesky(whole_block)]
    another operation x33 -> x0, local copies, waits for them, and re-layouts: 25.2 us -> none
    all_gather x2 -> x0, local copies, waits for them, and re-layouts: 14.5 us -> none  [the longest x1 8.99 us: body(): whole_rows = lax.all_gather(normals, 'cols', axis=1, tiled=True)]
  transfers between devices with their start and end apart: 6 -> 7, of which waited for: 5 -> 5; matrix products, arithmetic and copies ran while one was open for 3% -> 9% of each run, Pallas kernels for 0% -> 13%
where the time goes in v1:
time: 467 us; the launch traced here: 466 us
  waiting for transfers between devices  309 us (66%)
  Pallas kernels  61.5 us (13%)
  matrix products  28.9 us (6%)
  local copies, waits for them, and re-layouts  27.2 us (6%)
  other arithmetic  22.2 us (5%)
  between operations  14.4 us (3%)
    all_gather x1, waiting for transfers between devices, body(): gathered = lax.all_gather(filtered, 'cols', axis=1, tiled=True)  83.2 us
    reduce_scatter x1, waiting for transfers between devices, body(): lax.psum_scatter(lax.dot_general(gathered, filtered, contract, preferred_...  83.2 us
    pallas_call x1, Pallas kernels, inverse_factor_transposed(): pl.pallas_call(factor_kernel, out_shape=jax.ShapeDtypeStruct((size, size)...  61.5 us
    all_gather x1, waiting for transfers between devices, body(): pieces = lax.all_gather(piece, ('track', 'cols'), axis=0)  58.4 us
    reduce_scatter x1, waiting for transfers between devices, body(): lax.psum_scatter(own_part, 'track', scatter_dimension=0, tiled=True)  49.9 us
    reduce_scatter x1, waiting for transfers between devices, body(): piece = lax.psum_scatter(part, 'track', scatter_dimension=0, tiled=True)  34.6 us
    convert_element_type x1, other arithmetic, filter_rows(): coefs = jnp.where(col_rows >= starts, skewed, 0.0).astype(jnp.bfloat16)  13.1 us
    dot_general x1, matrix products, body(): lax.dot_general(gathered, filtered, contract, preferred_element_type=jnp....  10.7 us
  transfers between devices with their start and end apart: 7, of which 5 were waited for; matrix products, arithmetic and copies ran while one was open for 9% of the time, Pallas kernels for 13%

profile of v1, /device:TPU:0, one launch (start us, length us, event | category | flops | bytes accessed | tf_op | source)
XLA Modules:
  0.0 466.5 jit_solution(13285120891984932387)
XLA Ops:
  7.2 0.0 copy-start
  7.2 0.0 copy-start.8
  7.2 0.0 all-gather.5.cloned.1.call-start
  7.2 0.9 slice.16
  8.2 2.4 collective-permute-start
  10.6 0.1 ge.34
  10.7 1.9 ge.35
  12.6 0.0 copy-done.8
  12.6 0.0 copy-start.9
  12.6 0.1 ge.36
  12.8 2.9 ge.37
  15.7 0.0 copy-done
  15.7 0.0 copy-done.9
  15.7 0.3 fusion.10
  16.0 0.2 rev.3
  16.2 0.1 copy.11
  16.4 0.1 pad.4.clone
  16.4 1.4 reshape.105
  17.9 13.1 %fusion.6 = bf16[311296]{0:T(1024)(128)(2,1)S(1)} fusion(bf16[1,311808]{1,0:T(2,128)(2,1)S(1)} %reshape.105, s32[1,311296]{1,0:T(1,128)S(1)} %ge.35, s32[1,311296]{1,0:T(1,128)} %ge.37), kind=kLoop, calls=%fused_computation.14 | loop fusion | flops 622592 | bytes 3735552 | tf_op jit(solution)/shard_map/convert_element_type | solution.py:41
  31.0 0.9 convert_element_type.21
  31.9 0.9 slice.23
  32.8 0.0 collective-permute-done
  32.8 1.2 fusion.7
  34.1 0.0 copy-start.7
  34.1 2.0 convolution_convert_fusion
  36.1 0.0 all-gather.5.cloned.1.call-update
  36.1 0.2 reduce-scatter.4.cloned.1.call-start
  36.3 0.0 copy-done.7
  36.3 83.2 %all-gather.5.cloned.1.call-done = bf16[512,4096]{1,0:T(8,128)(2,1)} async-done(((bf16[512,1024]{1,0:T(8,128)(2,1)}), bf16[512,4096]{1,0:T(8,128)(2,1)}) %all-gather.5.cloned.1.call-update) | async-done | bytes 4194320 | tf_op jit(solution)/shard_map/all_gather | solution.py:183
  119.5 6.8 %fusion.2 = bf16[512,1024]{1,0:T(8,128)(2,1)S(1)} fusion(bf16[512,4096]{1,0:T(8,128)(2,1)} %all-gather.5.cloned.1.call-done, s32[1024]{0:T(1024)S(1)} %get-tuple-element.11), kind=kOutput, calls=%fused_computation.9 | convolution fusion | flops 4299685888 | bytes 5246976 | tf_op jit(solution)/shard_map/dot_general | solution.py:191
  126.3 0.0 copy-start.4
  126.4 1.5 fusion.15
  127.8 0.0 reduce-scatter.4.cloned.1.call-update
  127.9 0.0 all-gather.9.cloned.1.call-start
  127.9 34.6 %reduce-scatter.4.cloned.1.call-done = f32[128,256]{1,0:T(8,128)} async-done(((f32[1024,256]{1,0:T(8,128)}), f32[128,256]{1,0:T(8,128)}) %reduce-scatter.4.cloned.1.call-update) | async-done | bytes 131088 | tf_op jit(solution)/shard_map/reduce_scatter | solution.py:200
  162.5 0.0 all-gather.9.cloned.1.call-update
  162.5 0.0 reduce-scatter.8.cloned.1.call-start
  162.5 0.0 copy-done.4
  162.6 6.2 %gather_fusion = f32[1024]{0:T(1024)S(1)} fusion(f32[4096]{0:T(1024)S(1)} %copy-done.4, s32[1024]{0:T(1024)S(1)} %get-tuple-element.10), kind=kCustom, calls=%fused_computation | custom fusion | bytes 12288 | tf_op jit(solution)/shard_map/jit(_take)/gather | solution.py:207
  168.7 58.4 %all-gather.9.cloned.1.call-done = f32[4096,256]{1,0:T(8,128)} async-done(((f32[128,256]{1,0:T(8,128)}), f32[4096,256]{1,0:T(8,128)}) %all-gather.9.cloned.1.call-update) | async-done | bytes 4194320 | tf_op jit(solution)/shard_map/all_gather | solution.py:201
  227.1 4.9 %copy.10 = f32[8,4,128,256]{3,1,2,0:T(4,128)S(1)} copy(f32[8,4,128,256]{3,2,1,0:T(8,128)} %bitcast.26) | data formatting | bytes 8388608 | tf_op jit(solution)/shard_map/reshape | solution.py:203
  232.0 1.0 copy.12
  233.0 2.6 select_add_fusion.a_ref
  235.6 1.1 copy-done.5
  236.7 3.3 fusion.17
  240.0 0.0 reduce-scatter.8.cloned.1.call-update
  240.0 0.0 all-gather.7.cloned.1.call-start
  240.1 0.1 dynamic_slice.14
  240.1 0.1 dynamic_slice.13
  240.2 49.9 %reduce-scatter.8.cloned.1.call-done = f32[512,256]{1,0:T(8,128)} async-done(((f32[4096,256]{1,0:T(8,128)}), f32[512,256]{1,0:T(8,128)}) %reduce-scatter.8.cloned.1.call-update) | async-done | bytes 524304 | tf_op jit(solution)/shard_map/reduce_scatter | solution.py:219
  290.1 2.0 select_add_fusion.2
  292.1 0.0 all-gather.7.cloned.1.call-update
  292.2 0.3 reduce-scatter.6.cloned.1.call-start
  292.4 0.0 copy-done.6
  292.4 10.7 %fusion.16 = f32[4096,1024]{1,0:T(8,128)} fusion(bf16[512,4096]{1,0:T(8,128)(2,1)} %all-gather.5.cloned.1.call-done, bf16[512,1024]{1,0:T(8,128)(2,1)S(1)} %copy-done.6), kind=kOutput, calls=%fused_computation.33 | convolution fusion | flops 4294967296 | bytes 22020096 | tf_op jit(solution)/shard_map/dot_general | solution.py:224
  303.1 0.0 reduce-scatter.6.cloned.1.call-update
  303.2 2.2 copy-done.2
  305.3 61.5 %shard_map.77 = f32[1024,1024]{1,0:T(8,128)S(1)} custom-call(f32[1024,1024]{1,0:T(8,128)S(1)} %copy-done.2), custom_call_target="tpu_custom_call" | custom-call | flops 60000002048 | bytes 8388608 | tf_op jit(solution)/shard_map/pallas_call | solution.py:156
  366.8 0.0 copy-start.3
  366.8 2.0 copy-done.3
  368.8 4.5 fusion.8
  373.3 83.2 %reduce-scatter.6.cloned.1.call-done = f32[512,1024]{1,0:T(8,128)} async-done(((f32[4096,1024]{1,0:T(8,128)}), f32[512,1024]{1,0:T(8,128)}) %reduce-scatter.6.cloned.1.call-update) | async-done | bytes 2097168 | tf_op jit(solution)/shard_map/reduce_scatter | solution.py:223
  456.5 3.2 select_add_fusion.1
  459.6 0.0 copy-done.1
  (11 shorter events, 0.1 us)
Async XLA Ops:
  7.2 8.5 %copy-start = (bf16[8,97]{1,0:T(8,128)(2,1)S(1)}, bf16[8,97]{1,0:T(8,128)(2,1)}, u32[]{:S(2)}) copy-start(bf16[8,97]{1,0:T(8,128)(2,1)} %param.9) | copy-start | bytes 4660
  7.2 5.4 %copy-start.8 = (s32[512]{0:T(512)S(1)}, s32[512]{0:T(512)}, u32[]{:S(2)}) copy-start(s32[512]{0:T(512)} %param.7) | copy-start | bytes 6148
  7.2 112.3 %all-gather.5.cloned.1.call-start = ((), (), s32[]{:S(2)}) async-start(), calls=%async_computation.3 | async-start | bytes 5242880 | tf_op jit(solution)/shard_map/all_gather | solution.py:183
  8.2 24.6 %collective-permute-start = (bf16[96,1024]{1,0:T(8,128)(2,1)S(1)}, bf16[96,1024]{1,0:T(8,128)(2,1)S(1)}, u32[]{:S(2)}, u32[]{:S(2)}) collective-permute-start(bf16[96,1024]{1,0:T(8,128)(2,1)S(1)} %slice.16), channel_id=1, source_target_pairs={{0,4},{4,8},{8,12},{12,16},{16,20},{20,24},{24,28},{1,5},{5,9},{9,... | collective-permute-start | bytes 589832 | tf_op jit(solution)/shard_map/ppermute | solution.py:16
  12.6 3.1 copy-start.9
  34.1 2.2 copy-start.7
  36.1 126.4 %reduce-scatter.4.cloned.1.call-start = ((), (), s32[]{:S(2)}) async-start(), calls=%async_computation.4 | async-start | bytes 1179648 | tf_op jit(solution)/shard_map/reduce_scatter | solution.py:200
  126.3 36.3 %copy-start.4 = (f32[4096]{0:T(1024)S(1)}, f32[4096]{0:T(1024)}, u32[]{:S(2)}) copy-start(f32[4096]{0:T(1024)} %param.10) | copy-start | bytes 49156
  127.9 99.3 %all-gather.9.cloned.1.call-start = ((), (), s32[]{:S(2)}) async-start(), calls=%async_computation.8 | async-start | bytes 4325376 | tf_op jit(solution)/shard_map/all_gather | solution.py:201
  162.5 127.6 %reduce-scatter.8.cloned.1.call-start = ((), (), s32[]{:S(2)}) async-start(), calls=%async_computation.6 | async-start | bytes 4718592 | tf_op jit(solution)/shard_map/reduce_scatter | solution.py:219
  233.0 3.7 copy-start.5
  240.0 52.5 %copy-start.6 = (bf16[512,1024]{1,0:T(8,128)(2,1)S(1)}, bf16[512,1024]{1,0:T(8,128)(2,1)}, u32[]{:S(2)}) copy-start(bf16[512,1024]{1,0:T(8,128)(2,1)} %convolution_convert_fusion) | copy-start | bytes 3145732
  240.0 128.8 %all-gather.7.cloned.1.call-start = ((), (), s32[]{:S(2)}) async-start(), calls=%async_computation.7 | async-start | bytes 2621440 | tf_op jit(solution)/shard_map/all_gather | solution.py:221
  292.2 164.3 %reduce-scatter.6.cloned.1.call-start = ((), (), s32[]{:S(2)}) async-start(), calls=%async_computation.5 | async-start | bytes 18874368 | tf_op jit(solution)/shard_map/reduce_scatter | solution.py:223
  303.1 2.2 copy-start.2
  366.8 2.0 copy-start.3
  368.8 90.8 %copy-start.1 = (bf16[8,97]{1,0:T(8,128)(2,1)S(1)}, bf16[8,97]{1,0:T(8,128)(2,1)}, u32[]{:S(2)}) copy-start(bf16[8,97]{1,0:T(8,128)(2,1)} %param.9) | copy-start | bytes 4660
Sparse Core Ops, SparseCore 0:
  36.2 83.2 all-gather.4
  128.0 34.4 reduce-scatter.3
  165.5 61.6 all-gather.8
  240.1 49.9 reduce-scatter.7
  292.3 45.6 all-gather.6
  341.4 115.0 reduce-scatter.5

commit v2 on v1

--- a/solution.py
+++ b/solution.py
@@ -174,63 +174,45 @@
 def body(design, seg_start, seg_table, taps, ridge, col_perm):
     row_count, width_dev = design.shape
     halo_rows = taps.shape[1] - 1
-    track_size = lax.axis_size("track")
-    cols_size = lax.axis_size("cols")
     track_index = lax.axis_index("track")
     col_index = lax.axis_index("cols")
     ext_top = shifted(design[row_count - halo_rows :], "track", 1)
     filtered = filter_rows(design, ext_top, seg_start, seg_table, taps, track_index * row_count)
     gathered = lax.all_gather(filtered, "cols", axis=1, tiled=True)
     slab = gathered.shape[1]
-    row_blk = slab // track_size
-    panel_blk = PANEL // cols_size
+    row_blk = slab // lax.axis_size("track")
+    panel_blk = PANEL // lax.axis_size("cols")
     panel_ids = col_perm[:PANEL]
-    own_ids = lax.dynamic_slice_in_dim(panel_ids, col_index * panel_blk, panel_blk)
 
     chosen = (jnp.arange(slab, dtype=jnp.int32)[:, None] == panel_ids[None, :]).astype(jnp.bfloat16)
     panel_filtered = jnp.dot(gathered, chosen, preferred_element_type=jnp.float32).astype(
         jnp.bfloat16
     )
-    own_filtered = lax.dynamic_slice_in_dim(panel_filtered, col_index * panel_blk, panel_blk, 1)
     contract = (((0,), (0,)), ((), ()))
 
-    part = lax.dot_general(
-        panel_filtered, own_filtered, contract, preferred_element_type=jnp.float32
-    )
-    piece = lax.psum_scatter(part, "track", scatter_dimension=0, tiled=True)
-    pieces = lax.all_gather(piece, ("track", "cols"), axis=0)
-    block = (
-        pieces.reshape(track_size, cols_size, PANEL // track_size, panel_blk)
-        .transpose(0, 2, 1, 3)
-        .reshape(PANEL, PANEL)
-    )
+    panel_all = lax.all_gather(panel_filtered, "track", axis=0, tiled=True)
+    rows_all = lax.all_to_all(gathered, "track", split_axis=1, concat_axis=0, tiled=True)
+    filtered, panel_all, rows_all = lax.optimization_barrier((filtered, panel_all, rows_all))
+    cols_all = lax.all_gather(filtered, "track", axis=0, tiled=True)
+
+    block = lax.dot_general(panel_all, panel_all, contract, preferred_element_type=jnp.float32)
     panel_ridge = jnp.take(ridge, panel_ids)
     ids = jnp.arange(PANEL, dtype=jnp.int32)
     block = block + jnp.where(ids[:, None] == ids[None, :], panel_ridge[:, None], 0.0)
-
-    gathered, filtered, own_filtered, block = lax.optimization_barrier(
-        (gathered, filtered, own_filtered, block)
-    )
     inverse_t = inverse_factor_transposed(block)
+
     row_ids = track_index * row_blk + jnp.arange(row_blk, dtype=jnp.int32)
     row_ridge = lax.dynamic_slice_in_dim(ridge, track_index * row_blk, row_blk)
-
-    own_part = lax.dot_general(gathered, own_filtered, contract, preferred_element_type=jnp.float32)
-    own_cols = lax.psum_scatter(own_part, "track", scatter_dimension=0, tiled=True)
-    own_cols = own_cols + jnp.where(row_ids[:, None] == own_ids[None, :], row_ridge[:, None], 0.0)
-    panel_rows = lax.all_gather(own_cols, "cols", axis=1, tiled=True)
-
-    sums = lax.psum_scatter(
-        lax.dot_general(gathered, filtered, contract, preferred_element_type=jnp.float32),
-        "track",
-        scatter_dimension=0,
-        tiled=True,
-    )
+    panel_rows = lax.dot_general(rows_all, panel_all, contract, preferred_element_type=jnp.float32)
+    panel_rows = panel_rows + jnp.where(
+        row_ids[:, None] == panel_ids[None, :], row_ridge[:, None], 0.0
+    )
+    own_inverse = lax.dynamic_slice_in_dim(inverse_t, col_index * panel_blk, panel_blk, 1)
+    factor = jnp.dot(panel_rows, own_inverse, precision=lax.Precision.HIGHEST)
+
+    sums = lax.dot_general(rows_all, cols_all, contract, preferred_element_type=jnp.float32)
     col_ids = col_index * width_dev + jnp.arange(width_dev, dtype=jnp.int32)
     normals = sums + jnp.where(row_ids[:, None] == col_ids[None, :], row_ridge[:, None], 0.0)
-
-    own_inverse = lax.dynamic_slice_in_dim(inverse_t, col_index * panel_blk, panel_blk, 1)
-    factor = jnp.dot(panel_rows, own_inverse, precision=lax.Precision.HIGHEST)
     return (normals, factor)
 
 

time: 467 us -> 328 us (0.70)
  waiting for transfers between devices: 309 us -> 93 us
  blocking collectives: 0 us -> 77.5 us
  matrix products: 28.9 us -> 46.2 us
  local copies, waits for them, and re-layouts: 27.2 us -> 18.5 us
  other arithmetic: 22.2 us -> 14.4 us
    reduce_scatter x3 -> x0, waiting for transfers between devices: 168 us -> none  [the longest x1 83.2 us: body(): lax.psum_scatter(lax.dot_general(gathered, filtered, contract, preferred_...]
    all_to_all x0 -> x1, blocking collectives: none -> 77.5 us  [body(): lax.all_to_all(gathered, 'track', split_axis=1, concat_axis=0, tiled=True)]
    all_gather x2, waiting for transfers between devices: 58.4 us -> 9.79 us  [the longest x1 9.79 us: body(): panel_all = lax.all_gather(panel_filtered, 'track', axis=0, tiled=True)]
    dot_general x3, matrix products: 15.4 us -> 33.3 us  [the longest x1 13.8 us: body(): lax.dot_general(panel_all, panel_all, contract, preferred_element_type=jn...]
    add x3 -> x0, other arithmetic: 7.82 us -> none  [the longest x1 3.19 us: body(): sums + jnp.where(row_ids[:, None] == col_ids[None, :], row_ridge[:, None]...]
    unnamed x22 -> x11, local copies, waits for them, and re-layouts: 6.49 us -> 0.16 us
    reshape x1 -> x0, local copies, waits for them, and re-layouts: 4.89 us -> none  [body(): pieces.reshape(track_size, cols_size, PANEL // track_size, panel_blk)]
  transfers between devices with their start and end apart: 7 -> 4, of which waited for: 5 -> 2; matrix products, arithmetic and copies ran while one was open for 9% -> 17% of each run, Pallas kernels for 13% -> 19%
where the time goes in v2:
time: 328 us
  waiting for transfers between devices  93 us (28%)
  blocking collectives  77.5 us (24%)
  Pallas kernels  61.7 us (19%)
  matrix products  46.2 us (14%)
  local copies, waits for them, and re-layouts  18.5 us (6%)
  other arithmetic  14.4 us (4%)
  between operations  14 us (4%)
    all_gather x1, waiting for transfers between devices, body(): gathered = lax.all_gather(filtered, 'cols', axis=1, tiled=True)  83.2 us
    all_to_all x1, blocking collectives, body(): lax.all_to_all(gathered, 'track', split_axis=1, concat_axis=0, tiled=True)  77.5 us
    pallas_call x1, Pallas kernels, inverse_factor_transposed(): pl.pallas_call(factor_kernel, out_shape=jax.ShapeDtypeStruct((size, size)...  61.7 us
    dot_general x1, matrix products, body(): lax.dot_general(panel_all, panel_all, contract, preferred_element_type=jn...  13.8 us
    convert_element_type x1, other arithmetic, filter_rows(): coefs = jnp.where(col_rows >= starts, skewed, 0.0).astype(jnp.bfloat16)  13.1 us
    dot_general x1, matrix products, body(): lax.dot_general(rows_all, cols_all, contract, preferred_element_type=jnp....  10.5 us
    all_gather x1, waiting for transfers between devices, body(): panel_all = lax.all_gather(panel_filtered, 'track', axis=0, tiled=True)  9.79 us
    dot_general x1, matrix products, body(): lax.dot_general(rows_all, panel_all, contract, preferred_element_type=jnp...  9.05 us
  transfers between devices with their start and end apart: 4, of which 2 were waited for; matrix products, arithmetic and copies ran while one was open for 17% of the time, Pallas kernels for 19%

profile of v2, /device:TPU:0, one launch (start us, length us, event | category | flops | bytes accessed | tf_op | source)
XLA Modules:
  0.0 327.9 jit_solution(14483333713040553231)
XLA Ops:
  7.2 0.0 copy-start
  7.2 0.0 copy-start.3
  7.2 0.0 all-gather.4.cloned.1.call-start
  7.2 0.9 slice.16
  8.2 2.4 collective-permute-start
  10.6 0.1 ge.34
  10.7 1.9 ge.35
  12.6 0.0 copy-done.3
  12.6 0.0 copy-start.4
  12.6 0.1 ge.36
  12.8 2.9 ge.37
  15.7 0.0 copy-done
  15.7 0.0 copy-done.4
  15.7 0.3 fusion.17
  16.0 0.2 rev.3
  16.2 0.1 copy.10
  16.4 0.1 pad.4.clone
  16.4 1.4 reshape.101
  17.9 13.1 %fusion.10 = bf16[311296]{0:T(1024)(128)(2,1)S(1)} fusion(bf16[1,311808]{1,0:T(2,128)(2,1)S(1)} %reshape.101, s32[1,311296]{1,0:T(1,128)S(1)} %ge.35, s32[1,311296]{1,0:T(1,128)} %ge.37), kind=kLoop, calls=%fused_computation.19 | loop fusion | flops 622592 | bytes 3735552 | tf_op jit(solution)/shard_map/convert_element_type | solution.py:41
  31.0 0.9 convert_element_type.21
  31.9 0.9 slice.23
  32.8 0.0 collective-permute-done
  32.8 1.2 fusion.11
  34.1 0.0 copy-start.2
  34.1 2.0 convolution_convert_fusion
  36.1 0.0 all-gather.4.cloned.1.call-update
  36.1 0.2 all-gather.6.cloned.1.call-start
  36.3 0.0 copy-done.2
  36.3 83.2 %all-gather.4.cloned.1.call-done = bf16[512,4096]{1,0:T(8,128)(2,1)} async-done(((bf16[512,1024]{1,0:T(8,128)(2,1)}), bf16[512,4096]{1,0:T(8,128)(2,1)}) %all-gather.4.cloned.1.call-update) | async-done | bytes 4194320 | tf_op jit(solution)/shard_map/all_gather | solution.py:181
  119.5 7.8 %fusion.6 = bf16[512,1024]{1,0:T(8,128)(2,1)} fusion(bf16[512,4096]{1,0:T(8,128)(2,1)} %all-gather.4.cloned.1.call-done, s32[1024]{0:T(1024)S(1)} %get-tuple-element.9), kind=kOutput, calls=%fused_computation.14 | convolution fusion | flops 4299685888 | bytes 5246976 | tf_op jit(solution)/shard_map/dot_general | solution.py:188
  127.3 0.0 all-gather.6.cloned.1.call-update
  127.4 0.0 all-gather.8.cloned.1.call-start
  127.4 2.6 copy.13
  130.0 77.5 %all_to_all.19 = bf16[512,8,512]{2,0,1:T(8,128)(2,1)} all-to-all(bf16[512,8,512]{2,0,1:T(8,128)(2,1)S(1)} %bitcast.25), channel_id=1, replica_groups=mesh['track'=8,'cols'=4] {'track'}, dimensions={1} | all-to-all | bytes 8388608 | tf_op jit(solution)/shard_map/all_to_all | solution.py:194
  207.5 0.0 copy-start.1
  207.5 9.8 %all-gather.6.cloned.1.call-done = bf16[4096,1024]{1,0:T(8,128)(2,1)} async-done(((bf16[512,1024]{1,0:T(8,128)(2,1)}), bf16[4096,1024]{1,0:T(8,128)(2,1)}) %all-gather.6.cloned.1.call-update) | async-done | bytes 8388624 | tf_op jit(solution)/shard_map/all_gather | solution.py:193
  217.3 0.0 all-gather.8.cloned.1.call-update
  217.3 0.0 copy-done.1
  217.3 6.2 %gather_fusion = f32[1024]{0:T(1024)S(1)} fusion(f32[4096]{0:T(1024)S(1)} %copy-done.1, s32[1024]{0:T(1024)S(1)} %get-tuple-element.8), kind=kCustom, calls=%fused_computation | custom fusion | bytes 12288 | tf_op jit(solution)/shard_map/jit(_take)/gather | solution.py:199
  223.5 0.1 dynamic_slice.6
  223.6 9.0 %fusion.23 = f32[512,1024]{1,0:T(8,128)S(1)} fusion(bf16[4096,512]{1,0:T(8,128)(2,1)} %bitcast.26, bf16[4096,1024]{1,0:T(8,128)(2,1)} %all-gather.6.cloned.1.call-done), kind=kOutput, calls=%fused_computation.39 | convolution fusion | flops 4294967296 | bytes 14680064 | tf_op jit(solution)/shard_map/dot_general | solution.py:206
  232.6 13.8 %select_add_fusion.a_ref = f32[1024,1024]{1,0:T(8,128)S(1)} fusion(f32[1024]{0:T(1024)S(1)} %and_select_fusion, bf16[4096,1024]{1,0:T(8,128)(2,1)} %all-gather.6.cloned.1.call-done), kind=kOutput, calls=%fused_computation.6 | convolution fusion | flops 8593080320 | bytes 12587008 | tf_op jit(solution)/shard_map/dot_general | solution.py:198
  246.4 61.7 %shard_map.77 = f32[1024,1024]{1,0:T(8,128)S(1)} custom-call(f32[1024,1024]{1,0:T(8,128)S(1)} %select_add_fusion.a_ref), custom_call_target="tpu_custom_call" | custom-call | flops 60000002048 | bytes 8388608 | tf_op jit(solution)/shard_map/pallas_call | solution.py:156
  308.1 2.8 fusion.2
  310.9 0.0 all-gather.8.cloned.1.call-done
  310.9 10.5 %select_add_fusion.1 = f32[512,1024]{1,0:T(8,128)} fusion(bf16[4096,512]{1,0:T(8,128)(2,1)} %bitcast.27, bf16[4096,1024]{1,0:T(8,128)(2,1)} %all-gather.8.cloned.1.call-done, f32[512]{0:T(512)S(1)} %dynamic_slice.6, s32[1024]{0:T(1024)S(1)} %iota_add_fusion, s32[512]{0:T(512)S(1)} %iota_add_fusion.2), kind=kOutput, calls=%fused_computation.11 | convolution fusion | flops 4296540160 | bytes 14688256 | tf_op jit(solution)/shard_map/dot_general | solution.py:213
  (5 shorter events, 0.0 us)
Async XLA Ops:
  7.2 8.5 %copy-start = (bf16[8,97]{1,0:T(8,128)(2,1)S(1)}, bf16[8,97]{1,0:T(8,128)(2,1)}, u32[]{:S(2)}) copy-start(bf16[8,97]{1,0:T(8,128)(2,1)} %param.9) | copy-start | bytes 4660
  7.2 5.4 %copy-start.3 = (s32[512]{0:T(512)S(1)}, s32[512]{0:T(512)}, u32[]{:S(2)}) copy-start(s32[512]{0:T(512)} %param.7) | copy-start | bytes 6148
  7.2 112.3 %all-gather.4.cloned.1.call-start = ((), (), s32[]{:S(2)}) async-start(), calls=%async_computation.1 | async-start | bytes 5242880 | tf_op jit(solution)/shard_map/all_gather | solution.py:181
  8.2 24.6 %collective-permute-start = (bf16[96,1024]{1,0:T(8,128)(2,1)S(1)}, bf16[96,1024]{1,0:T(8,128)(2,1)S(1)}, u32[]{:S(2)}, u32[]{:S(2)}) collective-permute-start(bf16[96,1024]{1,0:T(8,128)(2,1)S(1)} %slice.16), channel_id=1, source_target_pairs={{0,4},{4,8},{8,12},{12,16},{16,20},{20,24},{24,28},{1,5},{5,9},{9,... | collective-permute-start | bytes 589832 | tf_op jit(solution)/shard_map/ppermute | solution.py:16
  12.6 3.1 copy-start.4
  34.1 2.2 copy-start.2
  36.1 181.2 %all-gather.6.cloned.1.call-start = ((), (), s32[]{:S(2)}) async-start(), calls=%async_computation.2 | async-start | bytes 9437184 | tf_op jit(solution)/shard_map/all_gather | solution.py:193
  127.4 183.5 %all-gather.8.cloned.1.call-start = ((), (), s32[]{:S(2)}) async-start(), calls=%async_computation.3 | async-start | bytes 9437184 | tf_op jit(solution)/shard_map/all_gather | solution.py:196
  207.5 9.8 %copy-start.1 = (f32[4096]{0:T(1024)S(1)}, f32[4096]{0:T(1024)}, u32[]{:S(2)}) copy-start(f32[4096]{0:T(1024)} %param.10) | copy-start | bytes 49156
Sparse Core Ops, SparseCore 0:
  36.2 83.2 all-gather.3
  127.5 89.7 all-gather.5
  219.7 51.8 all-gather.7
